TPU v7x, 32 devices: a whole 2x2x4 slice. The times are simulated.
32 devices in a mesh: seq: 8 (over z, y), tp: 4 (over x, core).
Axes of the slice: x: 2, y: 2, z: 4, core: 2. Of those that a mesh axis runs over, the one named last changes fastest.
Arguments:
- x_in: bfloat16 [1024, 8192], P('seq', 'tp'), may hold values from -6 to 6
- gate_in: bfloat16 [1024, 8192], P('seq', 'tp'), may hold values from -6 to 6
- conv_weight: float32 [4, 8192], P(None, 'tp'), may hold values from -3 to 3
- conv_bias: float32 [8192], P('tp'), may hold values from -0.5 to 0.5
- x_weight: bfloat16 [8192, 544], P('tp'), may hold values from -0.0625 to 0.0625
- dt_weight: bfloat16 [512, 8192], P(None, 'tp'), may hold values from -0.25 to 0.25
- dt_bias: float32 [8192], P('tp'), may hold values from -5 to -2.5
- decay_rate: float32 [8192, 16], P('tp'), may hold values from 0 to 4
- skip_gain: float32 [8192], P('tp'), may hold values from 0.5 to 1.5
- out_weight: bfloat16 [8192, 4096], P('tp'), may hold values from -0.0625 to 0.0625
- residual_in: bfloat16 [1024, 4096], P(('seq', 'tp')), may hold values from -36 to 36
- norm_gain: float32 [4096], replicated, may hold values from 0.1 to 1.9
- expert_ids: int32 [1024, 2], P(('seq', 'tp')), may hold values from 0 to 7, all different within a row; in each aligned block of 32 rows (0 to 31, 32 to 63, ...) at most 12 rows name the same one
- gate_prob: float32 [1024, 2], P(('seq', 'tp')), may hold values from 0.1 to 1
- up_weight: bfloat16 [4096, 98304], P(None, ('seq', 'tp')), may hold values from -0.09375 to 0.09375
- down_weight: bfloat16 [98304, 4096], P(('seq', 'tp')), may hold values from -0.0546875 to 0.0546875
Outputs:
- mixer_out: bfloat16 [1024, 4096], P(('seq', 'tp'))
- layer_out: bfloat16 [1024, 4096], P(('seq', 'tp'))
Inputs may be any that keep to these rules, and one draw needn't show every extreme that they name: `expert_ids`: each row names two different experts. In each device's aligned block of 32 rows no expert is named by more than 12 rows, a bound that some block reaches.
All inputs are finite; a program needn't handle non-finite values.
Results may differ from a plain program's by a relative error of at most 0.007.
Values may be sent and summed in bfloat16 or wider, within the bound.
A program may use at most 192 MiB of HBM per device.

v0:
```python
import jax
import jax.numpy as jnp
from jax import lax
from jax.sharding import PartitionSpec as P

STATE = 16
DTRANK = 512
EXPERTS = 8


def shifted(value, axis, steps):
    count = lax.axis_size(axis)
    initial, last = (max(0, -steps), min(count, count - steps))
    return lax.ppermute(value, axis, [(source, source + steps) for source in range(initial, last)])


def prefix(part, axis, combine, identity):
    place = lax.axis_index(axis)
    gathered = jax.tree.map(lambda a: lax.all_gather(a, axis), part)
    state = jax.tree.map(lambda a, e: jnp.zeros_like(a) + jnp.asarray(e, a.dtype), part, identity)

    def one(hop, state):
        return combine(
            state, jax.tree.map(lambda a: lax.dynamic_index_in_dim(a, hop, 0, False), gathered)
        )

    return lax.fori_loop(0, place, one, state)


def chain_join(earlier, later):
    return (earlier[0] * later[0], later[0] * earlier[1] + later[1])


def recur_blocks(start_state, step_cols, drive_cols, entry_cols, readout_cols, negative_rate):

    def advance(carried, columns):
        step_row, drive_row, entry_row, readout_row = columns
        carried = (
            jnp.exp(step_row[:, None, :] * negative_rate[None]) * carried
            + entry_row[:, :, None] * drive_row[:, None, :]
        )
        return (carried, jnp.sum(readout_row[:, :, None] * carried, axis=1))

    return lax.scan(advance, start_state, (step_cols, drive_cols, entry_cols, readout_cols))


def by_position(values, blocks, span):
    return values.reshape(blocks, span, values.shape[1]).transpose(1, 0, 2)


def expert_share(arrived_flat, up_weight, down_weight):
    hidden = jax.nn.silu(
        jnp.dot(arrived_flat, up_weight, preferred_element_type=jnp.float32)
    ).astype(jnp.bfloat16)
    return jnp.dot(hidden, down_weight, preferred_element_type=jnp.float32).astype(jnp.bfloat16)


def per_device(
    x_in,
    gate_in,
    conv_weight,
    conv_bias,
    x_weight,
    dt_weight,
    dt_bias,
    decay_rate,
    skip_gain,
    out_weight,
    residual_in,
    norm_gain,
    expert_ids,
    gate_prob,
    up_weight,
    down_weight,
):
    tokens, channels = x_in.shape
    width = out_weight.shape[1]
    reach = conv_weight.shape[0] - 1
    rim_rows = shifted(x_in[tokens - reach :], "seq", 1)
    padded = jnp.concatenate([rim_rows, x_in], axis=0).astype(jnp.float32)
    conv_out = conv_bias[None, :] + sum(
        (
            conv_weight[offset][None, :] * padded[offset : offset + tokens]
            for offset in range(reach + 1)
        )
    )
    inner = jax.nn.silu(conv_out).astype(jnp.bfloat16)
    projected = lax.psum(jnp.dot(inner, x_weight, preferred_element_type=jnp.float32), "tp")
    dt_low = projected[:, :DTRANK].astype(jnp.bfloat16)
    entry_rows = projected[:, DTRANK : DTRANK + STATE]
    readout_rows = projected[:, DTRANK + STATE :]
    step_size = jax.nn.softplus(
        jnp.dot(dt_low, dt_weight, preferred_element_type=jnp.float32) + dt_bias[None, :]
    )
    drive = step_size * inner.astype(jnp.float32)
    negative_rate = -decay_rate.T
    span = 16
    blocks = tokens // span
    step_cols = by_position(step_size, blocks, span)
    drive_cols = by_position(drive, blocks, span)
    entry_cols = by_position(entry_rows, blocks, span)
    readout_cols = by_position(readout_rows, blocks, span)
    zero_blocks = jnp.zeros((blocks, STATE, channels), jnp.float32)
    block_ends, local_out = recur_blocks(
        zero_blocks, step_cols, drive_cols, entry_cols, readout_cols, negative_rate
    )
    block_decay = jnp.exp(negative_rate[None] * jnp.sum(step_cols, axis=0)[:, None, :])
    decay_through, state_through = lax.associative_scan(
        chain_join, (block_decay, block_ends), axis=0
    )
    ones_state = jnp.ones((STATE, channels), jnp.float32)
    zeros_state = jnp.zeros((STATE, channels), jnp.float32)
    entering = prefix(
        (decay_through[-1], state_through[-1]), "seq", chain_join, (ones_state, zeros_state)
    )[1]
    decay_before = jnp.concatenate([ones_state[None], decay_through[:-1]], axis=0)
    state_before = jnp.concatenate([zeros_state[None], state_through[:-1]], axis=0)
    block_starts = decay_before * entering[None] + state_before
    ssm_cols = recur_blocks(
        block_starts, step_cols, drive_cols, entry_cols, readout_cols, negative_rate
    )[1]
    ssm = ssm_cols.transpose(1, 0, 2).reshape(tokens, channels)
    mixed = (
        (ssm + skip_gain[None, :] * inner.astype(jnp.float32))
        * jax.nn.silu(gate_in.astype(jnp.float32))
    ).astype(jnp.bfloat16)
    rows = tokens // lax.axis_size("tp")
    mixer_sum = lax.psum_scatter(
        jnp.dot(mixed, out_weight, preferred_element_type=jnp.float32),
        "tp",
        scatter_dimension=0,
        tiled=True,
    )
    mixer_out = (mixer_sum + residual_in.astype(jnp.float32)).astype(jnp.bfloat16)
    mixer_wide = mixer_out.astype(jnp.float32)
    normed = (
        mixer_wide
        * lax.rsqrt(jnp.mean(mixer_wide * mixer_wide, axis=1, keepdims=True) + 1e-06)
        * norm_gain[None, :]
    ).astype(jnp.bfloat16)
    seq_count = lax.axis_size("seq")
    devices = seq_count * lax.axis_size("tp")
    seq_group = seq_count // EXPERTS
    capacity = 3 * rows // EXPERTS
    chosen = expert_ids.reshape(-1)
    expert_hits = (chosen[:, None] == jnp.arange(EXPERTS, dtype=jnp.int32)[None, :]).astype(
        jnp.int32
    )
    earlier_hits = jnp.cumsum(expert_hits, axis=0) - expert_hits
    slot_index = jnp.sum(earlier_hits * expert_hits, axis=1)
    target = chosen * capacity + slot_index
    placing = (jnp.arange(EXPERTS * capacity, dtype=jnp.int32)[:, None] == target[None, :]).astype(
        jnp.bfloat16
    )
    placing = jnp.sum(placing.reshape(EXPERTS * capacity, rows, 2), axis=2)
    slots_out = (
        jnp.dot(placing, normed, preferred_element_type=jnp.float32)
        .astype(jnp.bfloat16)
        .reshape(EXPERTS, capacity, width)
    )
    along_seq = jnp.repeat(slots_out, seq_group, axis=0)
    arrived_seq = lax.all_to_all(along_seq, "seq", split_axis=0, concat_axis=0, tiled=True)
    arrived_all = lax.all_gather(
        arrived_seq.reshape(1, seq_count * capacity, width), "tp", axis=0, tiled=True
    )
    arrived_flat = arrived_all.reshape(devices * capacity, width)
    summed = lax.psum_scatter(
        expert_share(arrived_flat, up_weight, down_weight).astype(jnp.float32).astype(jnp.bfloat16),
        "tp",
        scatter_dimension=0,
        tiled=True,
    ).astype(jnp.float32)
    home = lax.all_to_all(
        summed.reshape(seq_count, capacity, width).astype(jnp.bfloat16),
        "seq",
        split_axis=0,
        concat_axis=0,
        tiled=True,
    ).astype(jnp.float32)
    expert_out = jnp.sum(home.reshape(EXPERTS, seq_group, capacity, width), axis=1).reshape(
        EXPERTS * capacity, width
    )
    picked = jnp.take(expert_out, target, axis=0).reshape(rows, 2, width)
    layer_out = (mixer_wide + jnp.sum(picked * gate_prob[:, :, None], axis=1)).astype(jnp.bfloat16)
    return (mixer_out, layer_out)


def solution(mesh):
    return jax.shard_map(
        per_device,
        mesh=mesh,
        in_specs=(
            P("seq", "tp"),
            P("seq", "tp"),
            P(None, "tp"),
            P("tp"),
            P("tp", None),
            P(None, "tp"),
            P("tp"),
            P("tp", None),
            P("tp"),
            P("tp", None),
            P(("seq", "tp"), None),
            P(),
            P(("seq", "tp"), None),
            P(("seq", "tp"), None),
            P(None, ("seq", "tp")),
            P(("seq", "tp"), None),
        ),
        out_specs=(P(("seq", "tp"), None), P(("seq", "tp"), None)),
        check_vma=False,
    )
```

profile of v0, /device:TPU:0, one launch (start us, length us, event | category | flops | bytes accessed | tf_op | source)
XLA Modules:
  0.0 464.8 jit_solution(15491746981362353329)
XLA Ops:
  8.1 4.9 %collective-permute-start = (bf16[3,2048]{1,0:T(4,128)(2,1)S(1)}, bf16[3,2048]{1,0:T(4,128)(2,1)S(1)}, u32[]{:S(2)}, u32[]{:S(2)}) collective-permute-start(bf16[3,2048]{1,0:T(4,128)(2,1)S(1)} %slice.130), channel_id=1, source_target_pairs={{0,4},{4,8},{8,12},{12,16},{16,20},{20,24},{24,28},{1,5},{5,9},{9,... | collective-permute-start | bytes 36872 | tf_op jit(solution)/shard_map/ppermute | solution.py:14
  19.5 33.8 %all-reduce.16.cloned.1.call-done = f32[128,544]{0,1:T(8,128)} async-done(((f32[128,544]{0,1:T(8,128)}), f32[128,544]{0,1:T(8,128)}) %all-reduce.16.cloned.1.call-update) | async-done | bytes 278544 | tf_op jit(solution)/shard_map/psum | solution.py:88
  53.3 2.7 convert_multiply_fusion.2
  56.6 2.6 copy_bitcast_fusion
  60.6 22.9 %while.37 = (s32[]{:T(128)}, f32[8,16,2048]{2,1,0:T(8,128)S(1)}, f32[16,8,2048]{2,1,0:T(8,128)}, f32[16,2048]{1,0:T(8,128)S(1)}, f32[16,8,16]{2,1,0:T(8,128)S(1)...) while((s32[]{:T(128)}, f32[8,16,2048]{2,1,0:T(8,128)S(1)}, f32[16,8,2048]{2,1,0:T(8,128)}, ...), condition=%wide.region_3.4_spmd.clone, body=%wide.region_2.3_spmd.clone.sunk | while | flops 1310723 | bytes 2623079 | solution.py:44
  87.4 2.4 pad.48
  89.9 2.4 pad.49
  94.4 4.2 pad.102
  100.1 2.4 pad.42
  102.6 2.4 pad.43
  105.0 2.2 add_multiply_fusion.1
  107.3 2.4 pad.50
  112.7 2.3 pad.104
  116.7 2.3 pad.45
  119.0 2.4 pad.67
  123.3 4.2 pad.44
  128.4 2.4 slice_add_fusion.5
  131.9 20.2 %all-gather.6.cloned.1.call-done = f32[8,16,2048]{2,1,0:T(8,128)} async-done(((f32[1,16,2048]{2,1,0:T(8,128)}), f32[8,16,2048]{2,1,0:T(8,128)}) %all-gather.6.cloned.1.call-update) | async-done | bytes 1048592 | tf_op jit(solution)/shard_map/all_gather | solution.py:19
  152.1 41.6 %all-gather.4.cloned.1.call-done = f32[8,16,2048]{2,1,0:T(8,128)} async-done(((f32[1,16,2048]{2,1,0:T(8,128)}), f32[8,16,2048]{2,1,0:T(8,128)}) %all-gather.4.cloned.1.call-update) | async-done | bytes 1048592 | tf_op jit(solution)/shard_map/all_gather | solution.py:19
  195.3 36.9 %while.36 = (s32[]{:T(128)}, f32[8,16,2048]{2,1,0:T(8,128)S(1)}, f32[16,8,2048]{2,1,0:T(8,128)}, f32[16,8,2048]{2,1,0:T(8,128)}, f32[16,2048]{1,0:T(8,128)S(1)},...) while((s32[]{:T(128)}, f32[8,16,2048]{2,1,0:T(8,128)S(1)}, ...), condition=%wide.region_8.9_spmd, body=%wide.region_6.8_spmd.sunk | while | flops 1556482 | bytes 2821733 | solution.py:44
  235.1 9.5 %fusion.40 = f32[128,4096]{1,0:T(8,128)} fusion(bf16[128,2048]{1,0:T(8,128)(2,1)S(1)} %fusion.4, bf16[2048,4096]{1,0:T(8,128)(2,1)} %param.31), kind=kOutput, calls=%fused_computation.108 | convolution fusion | flops 2147483648 | bytes 19398656 | tf_op jit(solution)/shard_map/dot_general | solution.py:129
  245.6 36.9 %reduce-scatter.3.cloned.1.call-done = f32[32,4096]{1,0:T(8,128)} async-done(((f32[128,4096]{1,0:T(8,128)}), f32[32,4096]{1,0:T(8,128)}) %reduce-scatter.3.cloned.1.call-update) | async-done | bytes 524304 | tf_op jit(solution)/shard_map/reduce_scatter | solution.py:128
  285.0 31.1 %all_to_all.10 = bf16[8,12,4096]{2,1,0:T(8,128)(2,1)S(1)} all-to-all(bf16[8,12,4096]{2,1,0:T(8,128)(2,1)S(1)} %reshape_broadcast_in_dim_reshape.3), channel_id=1, replica_groups=mesh['seq'=8,'tp'=4] {'seq'}, dimensions={0} | all-to-all | bytes 1572864 | tf_op jit(solution)/shard_map/all_to_all | solution.py:162
  317.4 26.5 %all-gather.8.cloned.1.call-done = bf16[4,96,4096]{2,1,0:T(8,128)(2,1)} async-done(((bf16[1,96,4096]{2,1,0:T(8,128)(2,1)}), bf16[4,96,4096]{2,1,0:T(8,128)(2,1)}) %all-gather.8.cloned.1.call-update) | async-done | bytes 3145744 | tf_op jit(solution)/shard_map/all_gather | solution.py:163
  343.9 16.0 %multiply_convert_fusion.5 = bf16[384,3072]{1,0:T(8,128)(2,1)S(1)} fusion(bf16[384,4096]{1,0:T(8,128)(2,1)} %bitcast.97, bf16[4096,3072]{1,0:T(8,128)(2,1)} %param.36), kind=kOutput, calls=%fused_computation.16.clone.clone.1 | convolution fusion | flops 9669574656 | bytes 30670848 | tf_op jit(solution)/shard_map/dot_general | solution.py:53
  360.0 15.9 %convolution_convert_fusion = bf16[384,4096]{1,0:T(8,128)(2,1)} fusion(bf16[3072,4096]{1,0:T(8,128)(2,1)} %param.37, bf16[384,3072]{1,0:T(8,128)(2,1)S(1)} %multiply_convert_fusion.5), kind=kOutput, calls=%fused_computation.15 | convolution fusion | flops 9665249280 | bytes 30670848 | tf_op jit(solution)/shard_map/dot_general | solution.py:55
  375.9 38.1 %reduce-scatter.5.cloned.1.call-done = bf16[96,4096]{1,0:T(8,128)(2,1)} async-done(((bf16[384,4096]{1,0:T(8,128)(2,1)}), bf16[96,4096]{1,0:T(8,128)(2,1)}) %reduce-scatter.5.cloned.1.call-update) | async-done | bytes 786448 | tf_op jit(solution)/shard_map/reduce_scatter | solution.py:167
  414.0 2.2 convert_element_type.72
  416.2 5.5 %all-to-all-start.1 = ((bf16[8,12,4096]{2,1,0:T(8,128)(2,1)}), bf16[8,12,4096]{2,1,0:T(8,128)(2,1)S(1)}, u32[]{:S(2)}, u32[]{:S(2)}) async-start(bf16[8,12,4096]{2,1,0:T(8,128)(2,1)} %convert_element_type.72), calls=%async_computation.3 | async-start | bytes 2097152 | tf_op jit(solution)/shard_map/all_to_all | solution.py:173
  422.1 25.4 %all-to-all-done.1 = bf16[8,12,4096]{2,1,0:T(8,128)(2,1)S(1)} async-done(((bf16[8,12,4096]{2,1,0:T(8,128)(2,1)}), bf16[8,12,4096]{2,1,0:T(8,128)(2,1)S(1)}, u32[]{:S(2)}, u32[]{:S(2)}) %all-to-all-start.1) | async-done | bytes 786464 | tf_op jit(solution)/shard_map/all_to_all | solution.py:173
  448.8 2.9 gather_fusion
  453.4 2.9 multiply_reduce_fusion.1
  (230 shorter events, 98.5 us)
Async XLA Ops:
  7.2 10.8 %copy-start = (bf16[2048,544]{0,1:T(8,128)(2,1)S(1)}, bf16[2048,544]{0,1:T(8,128)(2,1)}, u32[]{:S(2)}) copy-start(bf16[2048,544]{0,1:T(8,128)(2,1)} %param.26) | copy-start | bytes 6684676
  7.2 46.1 %all-reduce.16.cloned.1.call-start = ((), (), s32[]{:S(2)}) async-start(), calls=%async_computation.4 | async-start | bytes 557056 | tf_op jit(solution)/shard_map/psum | solution.py:88
  8.1 6.3 %collective-permute-start = (bf16[3,2048]{1,0:T(4,128)(2,1)S(1)}, bf16[3,2048]{1,0:T(4,128)(2,1)S(1)}, u32[]{:S(2)}, u32[]{:S(2)}) collective-permute-start(bf16[3,2048]{1,0:T(4,128)(2,1)S(1)} %slice.130), channel_id=1, source_target_pairs={{0,4},{4,8},{8,12},{12,16},{16,20},{20,24},{24,28},{1,5},{5,9},{9,... | collective-permute-start | bytes 36872 | tf_op jit(solution)/shard_map/ppermute | solution.py:14
  14.0 3.1 copy-start.12
  14.0 3.1 copy-start.14
  15.6 3.8 copy-start.11
  15.7 37.6 %copy-start.19 = (f32[2048]{0:T(1024)S(1)}, f32[2048]{0:T(1024)}, u32[]{:S(2)}) copy-start(f32[2048]{0:T(1024)} %param.28) | copy-start | bytes 24580
  17.1 0.8 copy-start.2
  19.4 132.7 %all-gather.6.cloned.1.call-start = ((), (), s32[]{:S(2)}) async-start(), calls=%async_computation.6 | async-start | bytes 1179648 | tf_op jit(solution)/shard_map/all_gather | solution.py:19
  100.1 7.1 %copy-start.9 = (f32[1,16,2048]{2,1,0:T(8,128)S(1)}, f32[1,16,2048]{2,1,0:T(8,128)}, u32[]{:S(2)}) copy-start(f32[1,16,2048]{2,1,0:T(8,128)} %slice.154) | copy-start | bytes 393220
  111.4 82.4 %all-gather.4.cloned.1.call-start = ((), (), s32[]{:S(2)}) async-start(), calls=%async_computation.5 | async-start | bytes 1179648 | tf_op jit(solution)/shard_map/all_gather | solution.py:19
  116.6 165.9 %reduce-scatter.3.cloned.1.call-start = ((), (), s32[]{:S(2)}) async-start(), calls=%async_computation.7 | async-start | bytes 2621440 | tf_op jit(solution)/shard_map/reduce_scatter | solution.py:128
  116.7 11.8 %copy-start.3 = (f32[8,16,2048]{2,1,0:T(8,128)S(1)}, f32[8,16,2048]{2,1,0:T(8,128)}, u32[]{:S(2)}) copy-start(f32[8,16,2048]{2,1,0:T(8,128)} %pad.102) | copy-start | bytes 3145732
  121.4 9.4 %copy-start.4 = (f32[8,16,2048]{2,1,0:T(8,128)S(1)}, f32[8,16,2048]{2,1,0:T(8,128)}, u32[]{:S(2)}) copy-start(f32[8,16,2048]{2,1,0:T(8,128)} %pad.45) | copy-start | bytes 3145732
  128.4 2.4 copy-start.5
  130.8 63.1 %copy-start.6 = (f32[7,16,2048]{2,1,0:T(8,128)S(1)}, f32[7,16,2048]{2,1,0:T(8,128)}, u32[]{:S(2)}) copy-start(f32[7,16,2048]{2,1,0:T(8,128)} %slice_add_fusion.5) | copy-start | bytes 2752516
  195.3 38.8 %copy-start.8 = (bf16[128,2048]{1,0:T(8,128)(2,1)S(1)}, bf16[128,2048]{1,0:T(8,128)(2,1)}, u32[]{:S(2)}) copy-start(bf16[128,2048]{1,0:T(8,128)(2,1)} %param.23) | copy-start | bytes 1572868
  195.3 38.8 %copy-start.13 = (f32[1,2048]{1,0:T(1,128)S(1)}, f32[1,2048]{1,0:T(1,128)}, u32[]{:S(2)}) copy-start(f32[1,2048]{1,0:T(1,128)} %copy-done.12) | copy-start | bytes 24580
  195.3 38.8 %copy-start.15 = (f32[1,2048]{1,0:T(1,128)S(1)}, f32[1,2048]{1,0:T(1,128)}, u32[]{:S(2)}) copy-start(f32[1,2048]{1,0:T(1,128)} %copy-done.14) | copy-start | bytes 24580
  195.3 38.8 %copy-start.16 = (f32[2048]{0:T(1024)S(1)}, f32[2048]{0:T(1024)}, u32[]{:S(2)}) copy-start(f32[2048]{0:T(1024)} %param.25) | copy-start | bytes 24580
  195.3 38.8 %copy-start.20 = (f32[2048]{0:T(1024)S(1)}, f32[2048]{0:T(1024)}, u32[]{:S(2)}) copy-start(f32[2048]{0:T(1024)} %param.30) | copy-start | bytes 24580
  235.1 9.6 %copy-start.18 = (s32[32,2]{0,1:T(2,128)S(1)}, s32[32,2]{0,1:T(2,128)}, u32[]{:S(2)}) copy-start(s32[32,2]{0,1:T(2,128)} %param.34) | copy-start | bytes 772
  235.1 47.3 %copy-start.10 = (bf16[32,4096]{1,0:T(8,128)(2,1)S(1)}, bf16[32,4096]{1,0:T(8,128)(2,1)}, u32[]{:S(2)}) copy-start(bf16[32,4096]{1,0:T(8,128)(2,1)} %param.32) | copy-start | bytes 786436
  244.6 39.7 %copy-start.17 = (f32[4096]{0:T(1024)S(1)}, f32[4096]{0:T(1024)}, u32[]{:S(2)}) copy-start(f32[4096]{0:T(1024)} %param.33) | copy-start | bytes 49156
  244.7 99.3 %all-gather.8.cloned.1.call-start = ((), (), s32[]{:S(2)}) async-start(), calls=%async_computation.8 | async-start | bytes 3932160 | tf_op jit(solution)/shard_map/all_gather | solution.py:163
  283.7 0.7 copy-start.7
  317.2 96.8 %reduce-scatter.5.cloned.1.call-start = ((), (), s32[]{:S(2)}) async-start(), calls=%async_computation.9 | async-start | bytes 3932160 | tf_op jit(solution)/shard_map/reduce_scatter | solution.py:167
  375.9 46.1 %copy-start.21 = (f32[32,2]{0,1:T(2,128)S(1)}, f32[32,2]{0,1:T(2,128)}, u32[]{:S(2)}) copy-start(f32[32,2]{0,1:T(2,128)} %param.35) | copy-start | bytes 772
  416.2 31.3 %all-to-all-start.1 = ((bf16[8,12,4096]{2,1,0:T(8,128)(2,1)}), bf16[8,12,4096]{2,1,0:T(8,128)(2,1)S(1)}, u32[]{:S(2)}, u32[]{:S(2)}) async-start(bf16[8,12,4096]{2,1,0:T(8,128)(2,1)} %convert_element_type.72), calls=%async_computation.3 | async-start | bytes 2097152 | tf_op jit(solution)/shard_map/all_to_all | solution.py:173
  448.8 9.1 %copy-start.1 = (bf16[2048,544]{0,1:T(8,128)(2,1)S(1)}, bf16[2048,544]{0,1:T(8,128)(2,1)}, u32[]{:S(2)}) copy-start(bf16[2048,544]{0,1:T(8,128)(2,1)} %param.26) | copy-start | bytes 6684676
Sparse Core Ops, SparseCore 0:
  19.5 33.7 all-reduce.15
  111.5 40.5 all-gather.5
  154.8 38.8 all-gather.3
  244.8 37.5 reduce-scatter.2
  317.3 26.5 all-gather.7
  376.0 37.9 reduce-scatter.4
where the time goes:
time: 467 us; the launch traced here: 465 us
  waiting for transfers between devices  223 us (48%)
  local copies, waits for them, and re-layouts  88.8 us (19%)
  other arithmetic  49.3 us (11%)
  matrix products  46.1 us (10%)
  blocking collectives  31.1 us (7%)
  between operations  14.6 us (3%)
  starting transfers between devices  10.9 us (2%)
    all_gather x2, waiting for transfers between devices, prefix(): gathered = jax.tree.map(lambda a: lax.all_gather(a, axis), part)  61.9 us
    reduce_scatter x1, waiting for transfers between devices, per_device(): lax.psum_scatter(expert_share(arrived_flat, up_weight, down_weight).astyp...  38.1 us
    reduce_scatter x1, waiting for transfers between devices, per_device(): lax.psum_scatter(jnp.dot(mixed, out_weight, preferred_element_type=jnp.fl...  36.9 us
    psum x1, waiting for transfers between devices, per_device(): lax.psum(jnp.dot(inner, x_weight, preferred_element_type=jnp.float32), 'tp')  33.8 us
    all_to_all x1, blocking collectives, per_device(): lax.all_to_all(along_seq, 'seq', split_axis=0, concat_axis=0, tiled=True)  31.1 us
    mul x48, local copies, waits for them, and re-layouts, advance(): entry_row[:, :, None] * drive_row[:, None, :]  28.5 us
    all_gather x1, waiting for transfers between devices, per_device(): lax.all_gather(arrived_seq.reshape(1, seq_count * capacity, width), 'tp',...  26.5 us
    all_to_all x1, waiting for transfers between devices, per_device(): lax.all_to_all(summed.reshape(seq_count, capacity, width).astype(jnp.bflo...  25.4 us
  transfers between devices with their start and end apart: 8, of which 8 were waited for; matrix products, arithmetic and copies ran while one was open for 5% of the time, Pallas kernels for 0%

commit v1 on v0

--- a/solution.py
+++ b/solution.py
@@ -6,6 +6,26 @@
 STATE = 16
 DTRANK = 512
 EXPERTS = 8
+
+
+def use_edge(sheet, dim_at):
+    u_next = list(sheet.shape[1:])
+    u_next[dim_at] *= sheet.shape[0]
+    return jnp.moveaxis(sheet, 0, dim_at).reshape(u_next)
+
+
+def cover_rows(block_in, peer_axis):
+    p_count = lax.psum(1, axis_name=peer_axis)
+    row_out = block_in[None]
+    for src_i in range(p_count.bit_length() - 1):
+        high = 1 << src_i
+        h_now = lax.ppermute(
+            row_out, axis_name=peer_axis, perm=tuple(((m, m ^ high) for m in range(p_count)))
+        )
+        side_arr = jnp.stack([row_out, h_now])
+        new = lax.axis_index(peer_axis) >> src_i & 1
+        row_out = jnp.where(new == 0, side_arr, side_arr[::-1]).reshape(-1, *block_in.shape)
+    return row_out
 
 
 def shifted(value, axis, steps):
@@ -160,9 +180,11 @@
     )
     along_seq = jnp.repeat(slots_out, seq_group, axis=0)
     arrived_seq = lax.all_to_all(along_seq, "seq", split_axis=0, concat_axis=0, tiled=True)
-    arrived_all = lax.all_gather(
-        arrived_seq.reshape(1, seq_count * capacity, width), "tp", axis=0, tiled=True
-    )
+
+    def _set_panel(x0, frame, pos_dim):
+        return use_edge(cover_rows(x0, frame), pos_dim)
+
+    arrived_all = _set_panel(arrived_seq.reshape(1, seq_count * capacity, width), "tp", 0)
     arrived_flat = arrived_all.reshape(devices * capacity, width)
     summed = lax.psum_scatter(
         expert_share(arrived_flat, up_weight, down_weight).astype(jnp.float32).astype(jnp.bfloat16),

time: 467 us -> 483 us (1.034)
  waiting for transfers between devices: 223 us -> 233 us
  other arithmetic: 49.3 us -> 54.2 us
    ppermute x0 -> x2, waiting for transfers between devices: none -> 38.1 us  [cover_rows(): lax.ppermute(row_out, axis_name=peer_axis, perm=tuple(((m, m ^ high) for...]
    all_gather x1 -> x0, waiting for transfers between devices: 26.5 us -> none  [per_device(): lax.all_gather(arrived_seq.reshape(1, seq_count * capacity, width), 'tp',...]
    another operation x0 -> x3, other arithmetic: none -> 5.08 us  [cover_rows(): side_arr = jnp.stack([row_out, h_now])]
  transfers between devices with their start and end apart: 8 -> 9, of which waited for: 8 -> 9; matrix products, arithmetic and copies ran while one was open for 5% -> 5% of each run, Pallas kernels for 0% -> 0%
where the time goes in v1:
time: 483 us; the launch traced here: 480 us
  waiting for transfers between devices  233 us (48%)
  local copies, waits for them, and re-layouts  90.1 us (19%)
  other arithmetic  54.2 us (11%)
  matrix products  45.2 us (9%)
  blocking collectives  31.1 us (6%)
  between operations  14.3 us (3%)
  starting transfers between devices  11.2 us (2%)
    all_gather x2, waiting for transfers between devices, prefix(): gathered = jax.tree.map(lambda a: lax.all_gather(a, axis), part)  61.8 us
    ppermute x2, waiting for transfers between devices, cover_rows(): lax.ppermute(row_out, axis_name=peer_axis, perm=tuple(((m, m ^ high) for...  38.1 us
    reduce_scatter x1, waiting for transfers between devices, per_device(): lax.psum_scatter(jnp.dot(mixed, out_weight, preferred_element_type=jnp.fl...  36.9 us
    reduce_scatter x1, waiting for transfers between devices, per_device(): lax.psum_scatter(expert_share(arrived_flat, up_weight, down_weight).astyp...  36.2 us
    psum x1, waiting for transfers between devices, per_device(): lax.psum(jnp.dot(inner, x_weight, preferred_element_type=jnp.float32), 'tp')  33.8 us
    all_to_all x1, blocking collectives, per_device(): lax.all_to_all(along_seq, 'seq', split_axis=0, concat_axis=0, tiled=True)  31.1 us
    mul x48, local copies, waits for them, and re-layouts, advance(): entry_row[:, :, None] * drive_row[:, None, :]  28.4 us
    all_to_all x1, waiting for transfers between devices, per_device(): lax.all_to_all(summed.reshape(seq_count, capacity, width).astype(jnp.bflo...  25.3 us
  transfers between devices with their start and end apart: 9, of which 9 were waited for; matrix products, arithmetic and copies ran while one was open for 5% of the time, Pallas kernels for 0%

profile of v1, /device:TPU:0, one launch (start us, length us, event | category | flops | bytes accessed | tf_op | source)
XLA Modules:
  0.0 479.7 jit_solution(2106598207567066338)
XLA Ops:
  8.1 4.9 %collective-permute-start = (bf16[3,2048]{1,0:T(4,128)(2,1)S(1)}, bf16[3,2048]{1,0:T(4,128)(2,1)S(1)}, u32[]{:S(2)}, u32[]{:S(2)}) collective-permute-start(bf16[3,2048]{1,0:T(4,128)(2,1)S(1)} %slice.130), channel_id=1, source_target_pairs={{0,4},{4,8},{8,12},{12,16},{16,20},{20,24},{24,28},{1,5},{5,9},{9,... | collective-permute-start | bytes 36872 | tf_op jit(solution)/shard_map/ppermute | solution.py:34
  19.4 33.8 %all-reduce.16.cloned.1.call-done = f32[128,544]{0,1:T(8,128)} async-done(((f32[128,544]{0,1:T(8,128)}), f32[128,544]{0,1:T(8,128)}) %all-reduce.16.cloned.1.call-update) | async-done | bytes 278544 | tf_op jit(solution)/shard_map/psum | solution.py:108
  53.2 2.7 convert_multiply_fusion.2
  56.5 2.6 copy_bitcast_fusion
  60.6 22.9 %while.37 = (s32[]{:T(128)}, f32[8,16,2048]{2,1,0:T(8,128)S(1)}, f32[16,8,2048]{2,1,0:T(8,128)}, f32[16,2048]{1,0:T(8,128)S(1)}, f32[16,8,16]{2,1,0:T(8,128)S(1)...) while((s32[]{:T(128)}, f32[8,16,2048]{2,1,0:T(8,128)S(1)}, f32[16,8,2048]{2,1,0:T(8,128)}, ...), condition=%wide.region_3.4_spmd.clone, body=%wide.region_2.3_spmd.clone.sunk | while | flops 1310723 | bytes 2623079 | solution.py:64
  87.5 2.4 pad.48
  89.9 2.4 pad.49
  94.4 4.2 pad.110
  100.2 2.4 pad.42
  102.6 2.4 pad.43
  105.1 2.3 add_multiply_fusion.1
  107.4 2.4 pad.50
  112.8 2.3 pad.112
  116.8 2.5 pad.45
  119.3 4.1 pad.71
  124.3 4.1 pad.44
  128.6 2.3 slice_add_fusion.5
  132.0 20.2 %all-gather.5.cloned.1.call-done = f32[8,16,2048]{2,1,0:T(8,128)} async-done(((f32[1,16,2048]{2,1,0:T(8,128)}), f32[8,16,2048]{2,1,0:T(8,128)}) %all-gather.5.cloned.1.call-update) | async-done | bytes 1048592 | tf_op jit(solution)/shard_map/all_gather | solution.py:39
  152.2 41.6 %all-gather.3.cloned.1.call-done = f32[8,16,2048]{2,1,0:T(8,128)} async-done(((f32[1,16,2048]{2,1,0:T(8,128)}), f32[8,16,2048]{2,1,0:T(8,128)}) %all-gather.3.cloned.1.call-update) | async-done | bytes 1048592 | tf_op jit(solution)/shard_map/all_gather | solution.py:39
  195.4 37.0 %while.36 = (s32[]{:T(128)}, f32[8,16,2048]{2,1,0:T(8,128)S(1)}, f32[16,8,2048]{2,1,0:T(8,128)}, f32[16,8,2048]{2,1,0:T(8,128)}, f32[16,2048]{1,0:T(8,128)S(1)},...) while((s32[]{:T(128)}, f32[8,16,2048]{2,1,0:T(8,128)S(1)}, ...), condition=%wide.region_8.9_spmd, body=%wide.region_6.8_spmd.sunk | while | flops 1556482 | bytes 2821733 | solution.py:64
  235.4 9.5 %fusion.42 = f32[128,4096]{1,0:T(8,128)} fusion(bf16[128,2048]{1,0:T(8,128)(2,1)S(1)} %fusion.6, bf16[2048,4096]{1,0:T(8,128)(2,1)} %param.31), kind=kOutput, calls=%fused_computation.114 | convolution fusion | flops 2147483648 | bytes 19398656 | tf_op jit(solution)/shard_map/dot_general | solution.py:149
  245.8 36.9 %reduce-scatter.3.cloned.1.call-done = f32[32,4096]{1,0:T(8,128)} async-done(((f32[128,4096]{1,0:T(8,128)}), f32[32,4096]{1,0:T(8,128)}) %reduce-scatter.3.cloned.1.call-update) | async-done | bytes 524304 | tf_op jit(solution)/shard_map/reduce_scatter | solution.py:148
  284.8 31.1 %all_to_all.10 = bf16[8,12,4096]{2,1,0:T(8,128)(2,1)S(1)} all-to-all(bf16[8,12,4096]{2,1,0:T(8,128)(2,1)S(1)} %reshape_broadcast_in_dim_reshape.3), channel_id=1, replica_groups=mesh['seq'=8,'tp'=4] {'seq'}, dimensions={0} | all-to-all | bytes 1572864 | tf_op jit(solution)/shard_map/all_to_all | solution.py:182
  316.3 2.2 collective-permute-done.1
  322.0 35.9 %collective-permute-done.2 = bf16[2,1,96,4096]{3,2,0,1:T(8,128)(2,1)S(1)} collective-permute-done((bf16[2,1,96,4096]{3,2,0,1:T(8,128)(2,1)S(1)}, bf16[2,1,96,4096]{3,2,0,1:T(8,128)(2,1)S(1)}, u32[]{:S(2)}, u32[]{:S(2)}) %collective-permute-start.2) | collective-permute-done | bytes 1572896 | tf_op jit(solution)/shard_map/ppermute | solution.py:22
  362.0 15.2 %multiply_convert_fusion.5 = bf16[384,3072]{1,0:T(8,128)(2,1)S(1)} fusion(bf16[384,4096]{1,0:T(8,128)(2,1)S(1)} %bitcast.92, bf16[4096,3072]{1,0:T(8,128)(2,1)} %param.36), kind=kOutput, calls=%fused_computation.17.clone.clone.1 | convolution fusion | flops 9669574656 | bytes 30670848 | tf_op jit(solution)/shard_map/dot_general | solution.py:73
  377.2 15.8 %convolution_convert_fusion = bf16[384,4096]{1,0:T(8,128)(2,1)} fusion(bf16[3072,4096]{1,0:T(8,128)(2,1)} %param.37, bf16[384,3072]{1,0:T(8,128)(2,1)S(1)} %multiply_convert_fusion.5), kind=kOutput, calls=%fused_computation.15 | convolution fusion | flops 9665249280 | bytes 30670848 | tf_op jit(solution)/shard_map/dot_general | solution.py:75
  393.1 36.2 %reduce-scatter.5.cloned.1.call-done = bf16[96,4096]{1,0:T(8,128)(2,1)} async-done(((bf16[384,4096]{1,0:T(8,128)(2,1)}), bf16[96,4096]{1,0:T(8,128)(2,1)}) %reduce-scatter.5.cloned.1.call-update) | async-done | bytes 786448 | tf_op jit(solution)/shard_map/reduce_scatter | solution.py:189
  431.5 5.5 %all-to-all-start.1 = ((bf16[8,12,4096]{2,1,0:T(8,128)(2,1)}), bf16[8,12,4096]{2,1,0:T(8,128)(2,1)S(1)}, u32[]{:S(2)}, u32[]{:S(2)}) async-start(bf16[8,12,4096]{2,1,0:T(8,128)(2,1)} %convert_element_type.72), calls=%async_computation.3 | async-start | bytes 2097152 | tf_op jit(solution)/shard_map/all_to_all | solution.py:195
  437.4 25.3 %all-to-all-done.1 = bf16[8,12,4096]{2,1,0:T(8,128)(2,1)S(1)} async-done(((bf16[8,12,4096]{2,1,0:T(8,128)(2,1)}), bf16[8,12,4096]{2,1,0:T(8,128)(2,1)S(1)}, u32[]{:S(2)}, u32[]{:S(2)}) %all-to-all-start.1) | async-done | bytes 786464 | tf_op jit(solution)/shard_map/all_to_all | solution.py:195
  464.1 2.9 gather_fusion
  468.6 2.9 multiply_reduce_fusion.1
  (247 shorter events, 105.2 us)
Async XLA Ops:
  7.2 10.7 %copy-start = (bf16[2048,544]{0,1:T(8,128)(2,1)S(1)}, bf16[2048,544]{0,1:T(8,128)(2,1)}, u32[]{:S(2)}) copy-start(bf16[2048,544]{0,1:T(8,128)(2,1)} %param.26) | copy-start | bytes 6684676
  7.2 46.0 %all-reduce.16.cloned.1.call-start = ((), (), s32[]{:S(2)}) async-start(), calls=%async_computation.4 | async-start | bytes 557056 | tf_op jit(solution)/shard_map/psum | solution.py:108
  8.1 6.3 %collective-permute-start = (bf16[3,2048]{1,0:T(4,128)(2,1)S(1)}, bf16[3,2048]{1,0:T(4,128)(2,1)S(1)}, u32[]{:S(2)}, u32[]{:S(2)}) collective-permute-start(bf16[3,2048]{1,0:T(4,128)(2,1)S(1)} %slice.130), channel_id=1, source_target_pairs={{0,4},{4,8},{8,12},{12,16},{16,20},{20,24},{24,28},{1,5},{5,9},{9,... | collective-permute-start | bytes 36872 | tf_op jit(solution)/shard_map/ppermute | solution.py:34
  14.0 3.0 copy-start.16
  14.0 3.0 copy-start.18
  17.8 35.4 %copy-start.24 = (f32[2048]{0:T(1024)S(1)}, f32[2048]{0:T(1024)}, u32[]{:S(2)}) copy-start(f32[2048]{0:T(1024)} %param.28) | copy-start | bytes 24580
  19.3 132.9 %all-gather.5.cloned.1.call-start = ((), (), s32[]{:S(2)}) async-start(), calls=%async_computation.6 | async-start | bytes 1179648 | tf_op jit(solution)/shard_map/all_gather | solution.py:39
  83.6 33.2 %copy-start.2 = (f32[8,16,2048]{2,1,0:T(8,128)}, f32[8,16,2048]{2,1,0:T(8,128)S(1)}, u32[]{:S(2)}) copy-start(f32[8,16,2048]{2,1,0:T(8,128)S(1)} %multiply_exponential_fusion) | copy-start | bytes 3145732
  100.2 7.1 %copy-start.13 = (f32[1,16,2048]{2,1,0:T(8,128)S(1)}, f32[1,16,2048]{2,1,0:T(8,128)}, u32[]{:S(2)}) copy-start(f32[1,16,2048]{2,1,0:T(8,128)} %slice.154) | copy-start | bytes 393220
  107.4 4.1 copy-start.4
  111.5 82.4 %all-gather.3.cloned.1.call-start = ((), (), s32[]{:S(2)}) async-start(), calls=%async_computation.5 | async-start | bytes 1179648 | tf_op jit(solution)/shard_map/all_gather | solution.py:39
  112.8 10.7 %copy-start.10 = (f32[3,16,2048]{2,1,0:T(8,128)S(1)}, f32[3,16,2048]{2,1,0:T(8,128)}, u32[]{:S(2)}) copy-start(f32[3,16,2048]{2,1,0:T(8,128)} %get-tuple-element.196) | copy-start | bytes 1179652
  116.7 165.9 %reduce-scatter.3.cloned.1.call-start = ((), (), s32[]{:S(2)}) async-start(), calls=%async_computation.7 | async-start | bytes 2621440 | tf_op jit(solution)/shard_map/reduce_scatter | solution.py:148
  116.8 6.6 %slice-start = ((f32[8,16,2048]{2,1,0:T(8,128)}), f32[1,16,2048]{2,1,0:T(8,128)S(1)}, s32[]{:S(2)}) async-start(f32[8,16,2048]{2,1,0:T(8,128)} %copy-done.2), calls=%async_computation.9 | async-start | bytes 262144 | tf_op jit(solution)/shard_map/slice | solution.py:128
  119.3 9.1 %copy-start.21 = (f32[128,16]{0,1:T(8,128)S(1)}, f32[128,16]{0,1:T(8,128)}, u32[]{:S(2)}) copy-start(f32[128,16]{0,1:T(8,128)} %get-tuple-element.206) | copy-start | bytes 24580
  119.3 9.3 %copy-start.5 = (f32[8,16,2048]{2,1,0:T(8,128)S(1)}, f32[8,16,2048]{2,1,0:T(8,128)}, u32[]{:S(2)}) copy-start(f32[8,16,2048]{2,1,0:T(8,128)} %pad.110) | copy-start | bytes 3145732
  124.3 6.7 %copy-start.6 = (f32[8,16,2048]{2,1,0:T(8,128)S(1)}, f32[8,16,2048]{2,1,0:T(8,128)}, u32[]{:S(2)}) copy-start(f32[8,16,2048]{2,1,0:T(8,128)} %pad.45) | copy-start | bytes 3145732
  128.6 2.4 copy-start.7
  131.0 63.1 %copy-start.8 = (f32[7,16,2048]{2,1,0:T(8,128)S(1)}, f32[7,16,2048]{2,1,0:T(8,128)}, u32[]{:S(2)}) copy-start(f32[7,16,2048]{2,1,0:T(8,128)} %slice_add_fusion.5) | copy-start | bytes 2752516
  195.4 39.0 %copy-start.17 = (f32[1,2048]{1,0:T(1,128)S(1)}, f32[1,2048]{1,0:T(1,128)}, u32[]{:S(2)}) copy-start(f32[1,2048]{1,0:T(1,128)} %copy-done.16) | copy-start | bytes 24580
  195.4 39.0 %copy-start.19 = (f32[1,2048]{1,0:T(1,128)S(1)}, f32[1,2048]{1,0:T(1,128)}, u32[]{:S(2)}) copy-start(f32[1,2048]{1,0:T(1,128)} %copy-done.18) | copy-start | bytes 24580
  195.4 39.0 %copy-start.20 = (f32[2048]{0:T(1024)S(1)}, f32[2048]{0:T(1024)}, u32[]{:S(2)}) copy-start(f32[2048]{0:T(1024)} %param.25) | copy-start | bytes 24580
  195.4 39.0 %copy-start.25 = (f32[2048]{0:T(1024)S(1)}, f32[2048]{0:T(1024)}, u32[]{:S(2)}) copy-start(f32[2048]{0:T(1024)} %param.30) | copy-start | bytes 24580
  235.4 9.6 %copy-start.23 = (s32[32,2]{0,1:T(2,128)S(1)}, s32[32,2]{0,1:T(2,128)}, u32[]{:S(2)}) copy-start(s32[32,2]{0,1:T(2,128)} %param.34) | copy-start | bytes 772
  244.9 37.8 %copy-start.14 = (bf16[32,4096]{1,0:T(8,128)(2,1)S(1)}, bf16[32,4096]{1,0:T(8,128)(2,1)}, u32[]{:S(2)}) copy-start(bf16[32,4096]{1,0:T(8,128)(2,1)} %param.32) | copy-start | bytes 786436
  244.9 39.0 %copy-start.22 = (f32[4096]{0:T(1024)S(1)}, f32[4096]{0:T(1024)}, u32[]{:S(2)}) copy-start(f32[4096]{0:T(1024)} %param.33) | copy-start | bytes 49156
  244.9 184.4 %reduce-scatter.5.cloned.1.call-start = ((), (), s32[]{:S(2)}) async-start(), calls=%async_computation.8 | async-start | bytes 3932160 | tf_op jit(solution)/shard_map/reduce_scatter | solution.py:189
  316.1 2.5 collective-permute-start.1
  321.5 36.4 %collective-permute-start.2 = (bf16[2,1,96,4096]{3,2,0,1:T(8,128)(2,1)S(1)}, bf16[2,1,96,4096]{3,2,0,1:T(8,128)(2,1)S(1)}, u32[]{:S(2)}, u32[]{:S(2)}) collective-permute-start(bf16[2,1,96,4096]{3,2,0,1:T(8,128)(2,1)S(1)} %get-tuple-element.195), channel_id=1, source_target_pairs={{0,2},{1,3},{2,0},{3,1},{4,6},{5,7},{6,4},{7,5},{8,10},{9,11},{10,... | collective-permute-start | bytes 4718600 | tf_op jit(solution)/shard_map/ppermute | solution.py:22
  393.1 44.2 %copy-start.26 = (f32[32,2]{0,1:T(2,128)S(1)}, f32[32,2]{0,1:T(2,128)}, u32[]{:S(2)}) copy-start(f32[32,2]{0,1:T(2,128)} %param.35) | copy-start | bytes 772
  431.5 31.3 %all-to-all-start.1 = ((bf16[8,12,4096]{2,1,0:T(8,128)(2,1)}), bf16[8,12,4096]{2,1,0:T(8,128)(2,1)S(1)}, u32[]{:S(2)}, u32[]{:S(2)}) async-start(bf16[8,12,4096]{2,1,0:T(8,128)(2,1)} %convert_element_type.72), calls=%async_computation.3 | async-start | bytes 2097152 | tf_op jit(solution)/shard_map/all_to_all | solution.py:195
  464.1 9.1 %copy-start.1 = (bf16[2048,544]{0,1:T(8,128)(2,1)S(1)}, bf16[2048,544]{0,1:T(8,128)(2,1)}, u32[]{:S(2)}) copy-start(bf16[2048,544]{0,1:T(8,128)(2,1)} %param.26) | copy-start | bytes 6684676
  (5 other events, 6.1 us)
Sparse Core Ops, SparseCore 0:
  19.4 33.7 all-reduce.15
  111.6 40.5 all-gather.4
  154.9 38.8 all-gather.2
  245.0 37.5 reduce-scatter.2
  393.2 36.0 reduce-scatter.4
